TPU v7x, 32 devices: a whole 2x2x4 slice. The times are simulated.
32 devices in a mesh: dp: 8 (over z, y), tensor: 4 (over x, core).
Axes of the slice: x: 2, y: 2, z: 4, core: 2. Of those that a mesh axis runs over, the one named last changes fastest.
Arguments:
- tokens: bfloat16 [8, 1536, 768], P('dp'), may hold values from -6 to 6
- timesteps: int32 [8], P('dp'), may hold values from 0 to 999
- piece_starts: int32 [8, 3], P('dp'), may hold values from 0 to 1280, as said below
- step_table: bfloat16 [1000, 768], replicated, may hold values from -4 to 4
- first_gain: float32 [768], replicated, may hold values from 0.5 to 1.5
- first_shift: float32 [768], replicated, may hold values from -2 to 2
- w_query: bfloat16 [768, 768], P(None, 'tensor'), may hold values from -0.3125 to 0.3125
- b_query: float32 [768], P('tensor'), may hold values from -2 to 2
- w_key: bfloat16 [768, 768], P(None, 'tensor'), may hold values from -0.3125 to 0.3125
- w_value: bfloat16 [768, 768], P(None, 'tensor'), may hold values from -0.21875 to 0.21875
- b_value: float32 [768], P('tensor'), may hold values from -2 to 2
- w_out: bfloat16 [768, 768], P('tensor'), may hold values from -0.875 to 0.875
- b_out: float32 [768], replicated, may hold values from -2 to 2
- second_gain: float32 [768], replicated, may hold values from 0.5 to 1.5
- second_shift: float32 [768], replicated, may hold values from -2 to 2
- w_in: bfloat16 [768, 3072], P(None, 'tensor'), may hold values from -0.21875 to 0.21875
- b_in: float32 [3072], P('tensor'), may hold values from -2 to 2
- w_down: bfloat16 [3072, 768], P('tensor'), may hold values from -0.109375 to 0.109375
- b_down: float32 [768], replicated, may hold values from -2 to 2
- cotangent: bfloat16 [8, 1536, 768], P('dp'), may hold values from -6 to 6
Outputs:
- output: bfloat16 [8, 1536, 768], P('dp')
- grad_tokens: bfloat16 [8, 1536, 768], P('dp')
- grad_step_table: float32 [1000, 768], replicated
- grad_first_gain: float32 [768], replicated
- grad_first_shift: float32 [768], replicated
- grad_w_query: float32 [768, 768], P(None, 'tensor')
- grad_b_query: float32 [768], P('tensor')
- grad_w_key: float32 [768, 768], P(None, 'tensor')
- grad_w_value: float32 [768, 768], P(None, 'tensor')
- grad_b_value: float32 [768], P('tensor')
- grad_w_out: float32 [768, 768], P('tensor')
- grad_b_out: float32 [768], replicated
- grad_second_gain: float32 [768], replicated
- grad_second_shift: float32 [768], replicated
- grad_w_in: float32 [768, 3072], P(None, 'tensor')
- grad_b_in: float32 [3072], P('tensor')
- grad_w_down: float32 [3072, 768], P('tensor')
- grad_b_down: float32 [768], replicated
Inputs may be any that keep to these rules, and one draw needn't show every extreme that they name: `piece_starts`: piece k of a sequence starts between 2 * k * 256 and 2 * k * 256 + 256, so pieces of 256 tokens lie inside their sequence, in order, without intersection.
All inputs are finite; a program needn't handle non-finite values.
Results may differ from a plain program's by a relative error of at most 0.02.
Values may be sent and summed in bfloat16 or wider, within the bound.
No kernel may reach another device: no remote copies, remote signals or barrier semaphores. Data moves between devices by JAX's collectives and lax.ppermute only.
A program may use at most 128 MiB of HBM per device.

v0:
```python
import jax
import jax.numpy as jnp
from jax import lax
from jax.sharding import PartitionSpec as P

HD = 64
PIECE = 256
QB = 512
EPS = 1e-05


def inner_rows(left, right):
    return lax.dot_general(
        left, right, (((0,), (0,)), ((), ())), preferred_element_type=jnp.float32
    )


def times_trans(left, right):
    return lax.dot_general(
        left, right, (((1,), (1,)), ((), ())), preferred_element_type=jnp.float32
    )


def normalize(values, gain, shift):
    center = values - jnp.mean(values, axis=-1, keepdims=True)
    root = lax.rsqrt(jnp.mean(center * center, axis=-1, keepdims=True) + EPS)
    hat = center * root
    return (hat * gain + shift, hat, root)


def norm_back(grad_in, hat, root, gain):
    scaled = grad_in * gain
    return root * (
        scaled
        - jnp.mean(scaled, axis=-1, keepdims=True)
        - hat * jnp.mean(scaled * hat, axis=-1, keepdims=True)
    )


def piece_labels(starts, length):
    positions = jnp.arange(length, dtype=jnp.int32)
    inside = (positions[None, :] >= starts[:, None]) & (
        positions[None, :] < starts[:, None] + PIECE
    )
    numbers = jnp.arange(1, starts.shape[0] + 1, dtype=jnp.int32)
    return jnp.sum(jnp.where(inside, numbers[:, None], 0), axis=0)


def block_scores(query_block, keys3, labels_q, place_q, labels, positions):
    scores = jnp.einsum("qhd,khd->hqk", query_block, keys3, preferred_element_type=jnp.float32)
    allowed = (positions[None, :] <= place_q[:, None]) | (labels_q[:, None] == labels[None, :]) & (
        labels_q[:, None] > 0
    )
    return jnp.where(allowed[None], scores, -1e30)


def per_device(
    tokens,
    timesteps,
    piece_starts,
    step_table,
    first_gain,
    first_shift,
    w_query,
    b_query,
    w_key,
    w_value,
    b_value,
    w_out,
    b_out,
    second_gain,
    second_shift,
    w_in,
    b_in,
    w_down,
    b_down,
    cotangent,
):
    length = tokens.shape[1]
    heads_here = w_query.shape[1] // HD
    scale = HD ** (-0.5)
    nblocks = length // QB
    table_rows = step_table.shape[0]
    onehot = (jnp.arange(table_rows, dtype=jnp.int32) == timesteps[0]).astype(jnp.bfloat16)
    step_row = jnp.dot(onehot[None, :], step_table, preferred_element_type=jnp.float32)[0]
    stream = tokens[0].astype(jnp.float32) + step_row[None, :]
    first_out, hat_one, root_one = normalize(stream, first_gain, first_shift)
    normed_one = first_out.astype(jnp.bfloat16)
    queries = (
        (jnp.dot(normed_one, w_query, preferred_element_type=jnp.float32) + b_query) * scale
    ).astype(jnp.bfloat16)
    keys_b = jnp.dot(normed_one, w_key, preferred_element_type=jnp.float32).astype(jnp.bfloat16)
    values_b = (jnp.dot(normed_one, w_value, preferred_element_type=jnp.float32) + b_value).astype(
        jnp.bfloat16
    )
    positions = jnp.arange(length, dtype=jnp.int32)
    labels = piece_labels(piece_starts[0], length)
    query_blocks = queries.reshape(nblocks, QB, heads_here, HD)
    keys3 = keys_b.reshape(length, heads_here, HD)
    values3 = values_b.reshape(length, heads_here, HD)
    label_blocks = labels.reshape(nblocks, QB)
    place_blocks = positions.reshape(nblocks, QB)

    def forward_block(pieces):
        query_block, labels_q, place_q = pieces
        scores = block_scores(query_block, keys3, labels_q, place_q, labels, positions)
        top = jnp.max(scores, axis=-1, keepdims=True)
        weights = jnp.exp(scores - top)
        total = jnp.sum(weights, axis=-1, keepdims=True)
        probs_b = (weights / total).astype(jnp.bfloat16)
        mixed = jnp.einsum("hqk,khd->qhd", probs_b, values3, preferred_element_type=jnp.float32)
        return (mixed.astype(jnp.bfloat16), (top + jnp.log(total))[:, :, 0])

    mixed_blocks, log_totals = lax.map(forward_block, (query_blocks, label_blocks, place_blocks))
    mixed_flat = mixed_blocks.reshape(length, heads_here * HD)
    attn_part = jnp.dot(mixed_flat, w_out, preferred_element_type=jnp.float32)
    attn = lax.psum(attn_part.astype(jnp.bfloat16), "tensor").astype(jnp.float32) + b_out
    hidden_one = stream + attn
    second_out, hat_two, root_two = normalize(hidden_one, second_gain, second_shift)
    normed_two = second_out.astype(jnp.bfloat16)
    pre_act = jnp.dot(normed_two, w_in, preferred_element_type=jnp.float32) + b_in
    active = jax.nn.gelu(pre_act, approximate=True).astype(jnp.bfloat16)
    mlp_part = jnp.dot(active, w_down, preferred_element_type=jnp.float32)
    mlp = lax.psum(mlp_part.astype(jnp.bfloat16), "tensor").astype(jnp.float32) + b_down
    output = (hidden_one + mlp).astype(jnp.bfloat16)[None]
    grad_top = cotangent[0]
    grad_top_f = grad_top.astype(jnp.float32)
    g_b_down = jnp.sum(grad_top_f, axis=0)
    g_w_down = inner_rows(active, grad_top)
    grad_active = times_trans(grad_top, w_down)
    _, gelu_pull = jax.vjp(lambda value: jax.nn.gelu(value, approximate=True), pre_act)
    grad_pre = gelu_pull(grad_active)[0].astype(jnp.bfloat16)
    g_b_in = jnp.sum(grad_pre.astype(jnp.float32), axis=0)
    g_w_in = inner_rows(normed_two, grad_pre)
    grad_two = lax.psum(times_trans(grad_pre, w_in).astype(jnp.bfloat16), "tensor").astype(
        jnp.float32
    )
    g_second_gain = jnp.sum(grad_two * hat_two, axis=0)
    g_second_shift = jnp.sum(grad_two, axis=0)
    g_w_in, g_b_in, g_w_down, g_b_down, g_second_gain, g_second_shift = lax.psum(
        (g_w_in, g_b_in, g_w_down, g_b_down, g_second_gain, g_second_shift), "dp"
    )
    grad_hidden = grad_top_f + norm_back(grad_two, hat_two, root_two, second_gain)
    grad_hidden_b = grad_hidden.astype(jnp.bfloat16)
    g_b_out = jnp.sum(grad_hidden, axis=0)
    g_w_out = inner_rows(mixed_flat, grad_hidden_b)
    grad_mixed = times_trans(grad_hidden_b, w_out).astype(jnp.bfloat16)
    grad_mixed_blocks = grad_mixed.reshape(nblocks, QB, heads_here, HD)

    def backward_block(carry, pieces):
        acc_keys, acc_values = carry
        query_block, labels_q, place_q, log_total, grad_block = pieces
        scores = block_scores(query_block, keys3, labels_q, place_q, labels, positions)
        probs = jnp.exp(scores - log_total[:, :, None])
        probs_b = probs.astype(jnp.bfloat16)
        grad_probs = jnp.einsum(
            "qhd,khd->hqk", grad_block, values3, preferred_element_type=jnp.float32
        )
        centre = jnp.sum(probs * grad_probs, axis=-1, keepdims=True)
        grad_scores = (probs * (grad_probs - centre)).astype(jnp.bfloat16)
        grad_query = jnp.einsum(
            "hqk,khd->qhd", grad_scores, keys3, preferred_element_type=jnp.float32
        )
        acc_keys = acc_keys + jnp.einsum(
            "hqk,qhd->khd", grad_scores, query_block, preferred_element_type=jnp.float32
        )
        acc_values = acc_values + jnp.einsum(
            "hqk,qhd->khd", probs_b, grad_block, preferred_element_type=jnp.float32
        )
        return ((acc_keys, acc_values), grad_query.astype(jnp.bfloat16))

    zero_acc = jnp.zeros((length, heads_here, HD), jnp.float32)
    (acc_keys, acc_values), grad_query_blocks = lax.scan(
        backward_block,
        (zero_acc, zero_acc),
        (query_blocks, label_blocks, place_blocks, log_totals, grad_mixed_blocks),
    )
    grad_queries = grad_query_blocks.reshape(length, heads_here * HD) * scale
    grad_keys = acc_keys.reshape(length, heads_here * HD).astype(jnp.bfloat16)
    grad_values = acc_values.reshape(length, heads_here * HD).astype(jnp.bfloat16)
    g_b_query = jnp.sum(grad_queries.astype(jnp.float32), axis=0)
    g_b_value = jnp.sum(grad_values.astype(jnp.float32), axis=0)
    g_w_query = inner_rows(normed_one, grad_queries)
    g_w_key = inner_rows(normed_one, grad_keys)
    g_w_value = inner_rows(normed_one, grad_values)
    grad_one_part = (
        times_trans(grad_queries, w_query)
        + times_trans(grad_keys, w_key)
        + times_trans(grad_values, w_value)
    )
    grad_one = lax.psum(grad_one_part.astype(jnp.bfloat16), "tensor").astype(jnp.float32)
    g_first_gain = jnp.sum(grad_one * hat_one, axis=0)
    g_first_shift = jnp.sum(grad_one, axis=0)
    grad_stream = grad_hidden + norm_back(grad_one, hat_one, root_one, first_gain)
    grad_tokens = grad_stream.astype(jnp.bfloat16)[None]
    row_total = jnp.sum(grad_stream, axis=0)
    table_local = onehot.astype(jnp.float32)[:, None] * row_total[None, :]
    (
        g_w_query,
        g_b_query,
        g_w_key,
        g_w_value,
        g_b_value,
        g_w_out,
        g_b_out,
        g_first_gain,
        g_first_shift,
        g_table,
    ) = lax.psum(
        (
            g_w_query,
            g_b_query,
            g_w_key,
            g_w_value,
            g_b_value,
            g_w_out,
            g_b_out,
            g_first_gain,
            g_first_shift,
            table_local,
        ),
        "dp",
    )
    return (
        output,
        grad_tokens,
        g_table,
        g_first_gain,
        g_first_shift,
        g_w_query,
        g_b_query,
        g_w_key,
        g_w_value,
        g_b_value,
        g_w_out,
        g_b_out,
        g_second_gain,
        g_second_shift,
        g_w_in,
        g_b_in,
        g_w_down,
        g_b_down,
    )


def solution(mesh):
    in_specs = (
        P("dp", None, None),
        P("dp"),
        P("dp", None),
        P(),
        P(),
        P(),
        P(None, "tensor"),
        P("tensor"),
        P(None, "tensor"),
        P(None, "tensor"),
        P("tensor"),
        P("tensor", None),
        P(),
        P(),
        P(),
        P(None, "tensor"),
        P("tensor"),
        P("tensor", None),
        P(),
        P("dp", None, None),
    )
    out_specs = (
        P("dp", None, None),
        P("dp", None, None),
        P(),
        P(),
        P(),
        P(None, "tensor"),
        P("tensor"),
        P(None, "tensor"),
        P(None, "tensor"),
        P("tensor"),
        P("tensor", None),
        P(),
        P(),
        P(),
        P(None, "tensor"),
        P("tensor"),
        P("tensor", None),
        P(),
    )
    return jax.shard_map(
        per_device, mesh=mesh, in_specs=in_specs, out_specs=out_specs, check_vma=False
    )
```

profile of v0, /device:TPU:0, one launch (start us, length us, event | category | flops | bytes accessed | tf_op | source)
XLA Modules:
  0.0 734.9 jit_solution(14062246603834037431)
XLA Ops:
  9.7 2.2 fusion.55
  17.3 2.6 convolution_convert_fusion.5
  20.0 2.6 fusion.85
  22.6 25.1 %while.28 = (s32[]{:T(128)}, bf16[3,512,3,64]{1,3,2,0:T(8,128)(2,1)S(1)}, f32[3,3,512]{2,1,0:T(4,128)S(1)}, s32[3,512]{1,0:T(4,128)S(1)}, s32[3,512]{1,0:T(4,128...) while((s32[]{:T(128)}, ...), condition=%wide.region_6.7_spmd.clone, body=%wide.region_3.6_spmd.clone.sunk | while | flops 628456448 | bytes 33111156 | solution.py:114
  23.8 1.7 select_reduce_fusion.3
  25.6 2.6 fusion.171
  28.2 2.8 fusion.172
  32.2 1.7 select_reduce_fusion.3
  33.9 2.6 fusion.171
  36.6 2.8 fusion.172
  40.6 1.7 select_reduce_fusion.3
  42.3 2.6 fusion.171
  44.9 2.8 fusion.172
  48.5 3.4 convolution_convert_fusion.3
  52.8 57.6 %all-reduce.8.cloned.1.call-done = bf16[1536,768]{1,0:T(8,128)(2,1)} async-done(((bf16[1536,768]{1,0:T(8,128)(2,1)}), bf16[1536,768]{1,0:T(8,128)(2,1)}) %all-reduce.8.cloned.1.call-update) | async-done | bytes 2359312 | tf_op jit(solution)/shard_map/psum | solution.py:117
  110.4 3.5 fusion.99
  113.9 3.0 multiply_reduce_fusion.1
  117.0 1.8 add_convert_fusion.2
  120.2 2.1 fusion.103
  122.4 5.3 convert_reduce_fusion.3
  129.1 3.5 convolution_convert_fusion.1
  132.9 3.6 fusion.88
  136.5 7.2 convolution_convert_fusion.2
  143.7 44.8 %all-reduce.10.cloned.1.call-done = bf16[1536,768]{1,0:T(8,128)(2,1)} async-done(((bf16[1536,768]{1,0:T(8,128)(2,1)}), bf16[1536,768]{1,0:T(8,128)(2,1)}) %all-reduce.10.cloned.1.call-update) | async-done | bytes 2359312 | tf_op jit(solution)/shard_map/psum | solution.py:135
  188.5 6.4 fusion.82
  194.9 5.2 fusion.100
  200.2 2.2 copy-done.9
  202.4 1.8 convolution_convert_fusion.4
  207.4 72.0 %while.29 = (s32[]{:T(128)}, f32[1536,3,64]{0,2,1:T(8,128)}, f32[1536,3,64]{0,2,1:T(8,128)S(1)}, bf16[3,512,3,64]{1,3,2,0:T(8,128)(2,1)}, bf16[3,512,3,64]{1,3,2...) while((s32[]{:T(128)}, f32[1536,3,64]{0,2,1:T(8,128)}, ...), condition=%wide.region_16.17_spmd.clone, body=%wide.region_14.16_spmd.clone.sunk | while | flops 1542683648 | bytes 159318784 | solution.py:173
  208.9 1.4 fusion.182
  210.4 4.2 multiply_reduce_fusion.3
  214.6 4.0 multiply_convert_fusion.5
  218.6 4.4 fusion.184
  223.1 4.6 fusion.186
  227.7 3.7 fusion.185
  232.6 1.4 fusion.182
  234.1 4.2 multiply_reduce_fusion.3
  238.3 4.0 multiply_convert_fusion.5
  242.3 4.8 fusion.184
  247.1 4.6 fusion.186
  251.7 3.7 fusion.185
  256.6 1.4 fusion.182
  258.0 4.2 multiply_reduce_fusion.3
  262.3 4.0 multiply_convert_fusion.5
  266.3 4.8 fusion.184
  271.1 4.6 fusion.186
  275.7 3.7 fusion.185
  281.2 2.0 fusion.104
  284.3 2.3 add_convert_fusion
  286.9 6.1 fusion.106
  292.9 6.7 fusion.89
  299.6 1.4 fusion.107
  301.1 1.4 fusion.109
  302.5 1.4 fusion.108
  304.0 1.5 fusion.95
  305.5 75.6 %all-reduce.14.cloned.1.call-done = (bf16[1536,768]{1,0:T(8,128)(2,1)}, bf16[1536,768]{1,0:T(8,128)(2,1)}) async-done(((bf16[1536,768]{1,0:T(8,128)(2,1)}, bf16[1536,768]{1,0:T(8,128)(2,1)}), (bf16[1536,768]{1,0:T(8,128)(2,1)}, bf16[1536,768]{1,0:T(8,128)(2,1)})) %all-reduce.14.cloned.1.call-update) | async-done | bytes 4718608 | tf_op jit(solution)/shard_map/psum | solution.py:124
  381.1 4.6 fusion.83
  385.8 6.9 fusion.101
  392.7 1.9 broadcast_multiply_fusion
  396.0 39.6 %all-reduce = (f32[768]{0:T(1024)}, f32[768]{0:T(1024)}, f32[192]{0:T(256)}, f32[192]{0:T(256)}, f32[768]{0:T(1024)}, /*index=5*/f32[768]{0:T(1024)}, f32[768]{0:T(1024)}, f32[768]{0:T(1024)}, f32[768]{0:T(1024)}) all-reduce(f32[768]{0:T(1024)S(1)} %get-tuple-element.271, ...), channel_id=1, replica_groups=mesh['dp'=8,'tensor'=4] {'dp'}, use_global_device_ids=true, to_apply=%region_23.24 | all-reduce | flops 5760 | bytes 46080 | tf_op jit(solution)/shard_map/psum | solution.py:209
  435.6 282.6 %all-reduce.12.cloned.1.call-done = (f32[1000,768]{1,0:T(8,128)}, f32[768,192]{0,1:T(8,128)}, f32[768,192]{0,1:T(8,128)}, f32[768,192]{0,1:T(8,128)}, f32[192,76...) async-done(((f32[1000,768]{1,0:T(8,128)}, f32[768,192]{0,1:T(8,128)}, f32[768,192]{0,1:T(8,128)}, f32[768,192]{0,1:T(8,128)}, f32[192,768]{1,0:T(8,128)}, ...) | async-done | bytes 10149904 | tf_op jit(solution)/shard_map/psum | solution.py:209
  718.2 3.9 copy.89
  725.3 1.4 copy.94
  726.7 1.4 copy.95
  (219 shorter events, 29.7 us)
Async XLA Ops:
  7.2 2.1 copy-start
  7.2 5.7 copy-start.44
  7.2 5.7 copy-start.52
  7.2 103.2 %all-reduce.8.cloned.1.call-start = ((), (), s32[]{:S(2)}) async-start(), calls=%async_computation | async-start | bytes 4718592 | tf_op jit(solution)/shard_map/psum | solution.py:117
  7.3 4.6 copy-start.4
  9.6 6.1 copy-start.36
  9.7 6.0 copy-start.61
  11.9 120.9 %copy-start.34 = (f32[1536]{0:T(1024)}, f32[1536]{0:T(1024)S(1)}, u32[]{:S(2)}) copy-start(f32[1536]{0:T(1024)S(1)} %broadcast_multiply_fusion.7) | copy-start | bytes 18436
  12.9 119.9 %copy-start.41 = (f32[1536]{0:T(1024)}, f32[1536]{0:T(1024)S(1)}, u32[]{:S(2)}) copy-start(f32[1536]{0:T(1024)S(1)} %add_rsqrt_fusion.1) | copy-start | bytes 18436
  15.7 1.5 copy-start.37
  16.6 3.2 copy-start.56
  16.6 3.3 copy-start.39
  16.7 3.3 copy-start.62
  47.8 4.4 copy-start.11
  47.8 62.6 %copy-start.43 = (f32[768]{0:T(1024)S(1)}, f32[768]{0:T(1024)}, u32[]{:S(2)}) copy-start(f32[768]{0:T(1024)} %param.36) | copy-start | bytes 9220
  48.5 3.7 copy-start.16
  51.9 136.6 %all-reduce.10.cloned.1.call-start = ((), (), s32[]{:S(2)}) async-start(), calls=%async_computation.1 | async-start | bytes 4718592 | tf_op jit(solution)/shard_map/psum | solution.py:135
  52.8 64.2 %copy-start.46 = (f32[768]{0:T(1024)S(1)}, f32[768]{0:T(1024)}, u32[]{:S(2)}) copy-start(f32[768]{0:T(1024)} %param.37) | copy-start | bytes 9220
  52.8 64.2 %copy-start.53 = (f32[768]{0:T(1024)S(1)}, f32[768]{0:T(1024)}, u32[]{:S(2)}) copy-start(f32[768]{0:T(1024)} %param.38) | copy-start | bytes 9220
  110.4 3.5 copy-start.7
  110.4 6.6 copy-start.5
  117.0 3.3 copy-start.57
  120.2 2.1 copy-start.22
  120.2 2.1 copy-start.58
  120.2 2.1 copy-start.60
  122.4 5.3 copy-start.63
  132.6 248.5 %all-reduce.14.cloned.1.call-start = ((), (), s32[]{:S(2)}) async-start(), calls=%async_computation.3 | async-start | bytes 9437184 | tf_op jit(solution)/shard_map/psum | solution.py:124
  132.9 3.6 copy-start.59
  188.5 6.4 copy-start.6
  188.5 6.4 copy-start.8
  188.5 6.4 copy-start.15
  194.9 7.5 %copy-start.29 = (bf16[192,768]{1,0:T(8,128)(2,1)S(1)}, bf16[192,768]{1,0:T(8,128)(2,1)}, u32[]{:S(2)}) copy-start(bf16[192,768]{1,0:T(8,128)(2,1)} %param.35) | copy-start | bytes 884740
  200.2 2.2 copy-start.9
  210.4 4.3 copy-start.2
  218.6 9.1 %copy-start.3 = (f32[3,512,1536]{2,1,0:T(8,128)S(1)}, f32[3,512,1536]{2,1,0:T(8,128)}, u32[]{:S(2)}) copy-start(f32[3,512,1536]{2,1,0:T(8,128)} %copy-done.2) | copy-start | bytes 28311556 | tf_op jit(solution)/shard_map/while
  232.6 1.5 copy-start.12
  234.0 4.3 copy-start.2
  242.3 9.4 %copy-start.3 = (f32[3,512,1536]{2,1,0:T(8,128)S(1)}, f32[3,512,1536]{2,1,0:T(8,128)}, u32[]{:S(2)}) copy-start(f32[3,512,1536]{2,1,0:T(8,128)} %copy-done.2) | copy-start | bytes 28311556 | tf_op jit(solution)/shard_map/while
  258.0 4.3 copy-start.2
  266.3 9.4 %copy-start.3 = (f32[3,512,1536]{2,1,0:T(8,128)S(1)}, f32[3,512,1536]{2,1,0:T(8,128)}, u32[]{:S(2)}) copy-start(f32[3,512,1536]{2,1,0:T(8,128)} %copy-done.2) | copy-start | bytes 28311556 | tf_op jit(solution)/shard_map/while
  281.2 2.1 copy-start.19
  281.2 2.1 copy-start.10
  281.2 2.1 copy-start.38
  286.6 431.5 %all-reduce.12.cloned.1.call-start = ((), (), s32[]{:S(2)}) async-start(), calls=%async_computation.2 | async-start | bytes 20299776 | tf_op jit(solution)/shard_map/psum | solution.py:209
  286.8 6.1 copy-start.23
  292.9 6.7 copy-start.20
  292.9 6.7 copy-start.27
  299.6 4.3 slice-start
  301.1 2.9 slice-start.1
  301.1 2.9 copy-start.17
  302.5 78.6 %copy-start.35 = (f32[1536]{0:T(1024)S(1)}, f32[1536]{0:T(1024)}, u32[]{:S(2)}) copy-start(f32[1536]{0:T(1024)} %copy-done.34) | copy-start | bytes 18436
  302.5 78.6 %copy-start.42 = (f32[1536]{0:T(1024)S(1)}, f32[1536]{0:T(1024)}, u32[]{:S(2)}) copy-start(f32[1536]{0:T(1024)} %copy-done.41) | copy-start | bytes 18436
  302.5 78.6 %copy-start.45 = (f32[768]{0:T(1024)S(1)}, f32[768]{0:T(1024)}, u32[]{:S(2)}) copy-start(f32[768]{0:T(1024)} %param.28) | copy-start | bytes 9220
  304.0 81.8 %copy-start.54 = (f32[768]{0:T(1024)S(1)}, f32[768]{0:T(1024)}, u32[]{:S(2)}) copy-start(f32[768]{0:T(1024)} %param.42) | copy-start | bytes 9220
  381.1 4.7 copy-start.13
  381.1 4.7 copy-start.21
  385.8 6.9 copy-start.51
  718.2 3.9 copy-start.33
  718.2 4.7 copy-start.32
  718.2 5.5 copy-start.31
  718.2 6.3 copy-start.30
  718.2 7.1 copy-start.26
  722.0 4.7 copy-start.25
  724.5 3.6 copy-start.1
  (12 other events, 16.0 us)
Sparse Core Ops, SparseCore 0:
  52.0 58.3 all-reduce.7
  132.7 55.7 all-reduce.9
  286.7 94.2 all-reduce.13
  394.8 323.3 all-reduce.11
where the time goes:
time: 743 us; the launch traced here: 735 us
  waiting for transfers between devices  461 us (62%)
  matrix products  123 us (17%)
  other arithmetic  70.5 us (9%)
  blocking collectives  39.6 us (5%)
  local copies, waits for them, and re-layouts  24.2 us (3%)
  between operations  15.5 us (2%)
    psum x1, waiting for transfers between devices, per_device(): lax.psum((g_w_query, g_b_query, g_w_key, g_w_value, g_b_value, g_w_out, g...  283 us
    psum x1, waiting for transfers between devices, per_device(): lax.psum(mlp_part.astype(jnp.bfloat16), 'tensor').astype(jnp.float32)  75.6 us
    psum x1, waiting for transfers between devices, per_device(): lax.psum(attn_part.astype(jnp.bfloat16), 'tensor').astype(jnp.float32)  57.6 us
    psum x1, waiting for transfers between devices, per_device(): lax.psum(times_trans(grad_pre, w_in).astype(jnp.bfloat16), 'tensor')  44.8 us
    psum x1, blocking collectives, per_device(): lax.psum((g_w_query, g_b_query, g_w_key, g_w_value, g_b_value, g_w_out, g...  39.6 us
    unnamed x137, local copies, waits for them, and re-layouts  20.1 us
    dot_general x6, matrix products, inner_rows(): lax.dot_general(left, right, (((0,), (0,)), ((), ())), preferred_element_...  18.6 us
    dot_general x6, matrix products, times_trans(): lax.dot_general(left, right, (((1,), (1,)), ((), ())), preferred_element_...  15.7 us
  transfers between devices with their start and end apart: 4, of which 4 were waited for; matrix products, arithmetic and copies ran while one was open for 4% of the time, Pallas kernels for 0%

commit v1 on v0

--- a/solution.py
+++ b/solution.py
@@ -132,9 +132,9 @@
     grad_pre = gelu_pull(grad_active)[0].astype(jnp.bfloat16)
     g_b_in = jnp.sum(grad_pre.astype(jnp.float32), axis=0)
     g_w_in = inner_rows(normed_two, grad_pre)
-    grad_two = lax.psum(times_trans(grad_pre, w_in).astype(jnp.bfloat16), "tensor").astype(
-        jnp.float32
-    )
+    grad_two = jnp.sum(
+        lax.all_gather(times_trans(grad_pre, w_in).astype(jnp.bfloat16), "tensor"), 0
+    ).astype(jnp.float32)
     g_second_gain = jnp.sum(grad_two * hat_two, axis=0)
     g_second_shift = jnp.sum(grad_two, axis=0)
     g_w_in, g_b_in, g_w_down, g_b_down, g_second_gain, g_second_shift = lax.psum(

time: 743 us -> 761 us (1.024)
  other arithmetic: 70.5 us -> 79 us
  waiting for transfers between devices: 461 us -> 469 us
    all_gather x0 -> x1, waiting for transfers between devices: none -> 52.9 us  [per_device(): lax.all_gather(times_trans(grad_pre, w_in).astype(jnp.bfloat16), 'tensor')]
    psum x1 -> x0, waiting for transfers between devices: 44.8 us -> none  [per_device(): lax.psum(times_trans(grad_pre, w_in).astype(jnp.bfloat16), 'tensor')]
    unnamed x137 -> x135, local copies, waits for them, and re-layouts: 20.1 us -> 20.1 us
where the time goes in v1:
time: 761 us; the launch traced here: 752 us
  waiting for transfers between devices  469 us (62%)
  matrix products  123 us (16%)
  other arithmetic  79 us (10%)
  blocking collectives  39.6 us (5%)
  local copies, waits for them, and re-layouts  24.2 us (3%)
  between operations  15.5 us (2%)
    psum x1, waiting for transfers between devices, per_device(): lax.psum((g_w_query, g_b_query, g_w_key, g_w_value, g_b_value, g_w_out, g...  283 us
    psum x1, waiting for transfers between devices, per_device(): lax.psum(mlp_part.astype(jnp.bfloat16), 'tensor').astype(jnp.float32)  75.6 us
    psum x1, waiting for transfers between devices, per_device(): lax.psum(attn_part.astype(jnp.bfloat16), 'tensor').astype(jnp.float32)  58.2 us
    all_gather x1, waiting for transfers between devices, per_device(): lax.all_gather(times_trans(grad_pre, w_in).astype(jnp.bfloat16), 'tensor')  52.9 us
    psum x1, blocking collectives, per_device(): lax.psum((g_w_query, g_b_query, g_w_key, g_w_value, g_b_value, g_w_out, g...  39.6 us
    unnamed x135, local copies, waits for them, and re-layouts  20.1 us
    dot_general x6, matrix products, inner_rows(): lax.dot_general(left, right, (((0,), (0,)), ((), ())), preferred_element_...  18.5 us
    dot_general x6, matrix products, times_trans(): lax.dot_general(left, right, (((1,), (1,)), ((), ())), preferred_element_...  15.6 us
  transfers between devices with their start and end apart: 4, of which 4 were waited for; matrix products, arithmetic and copies ran while one was open for 4% of the time, Pallas kernels for 0%

profile of v1, /device:TPU:0, one launch (start us, length us, event | category | flops | bytes accessed | tf_op | source)
XLA Modules:
  0.0 751.9 jit_solution(17602325179279647837)
XLA Ops:
  9.7 2.2 fusion.55
  17.3 2.6 convolution_convert_fusion.5
  20.0 2.6 fusion.85
  22.6 25.1 %while.28 = (s32[]{:T(128)}, bf16[3,512,3,64]{1,3,2,0:T(8,128)(2,1)S(1)}, f32[3,3,512]{2,1,0:T(4,128)S(1)}, s32[3,512]{1,0:T(4,128)S(1)}, s32[3,512]{1,0:T(4,128...) while((s32[]{:T(128)}, ...), condition=%wide.region_6.7_spmd.clone, body=%wide.region_3.6_spmd.clone.sunk | while | flops 628456448 | bytes 33111156 | solution.py:114
  23.8 1.7 select_reduce_fusion.3
  25.6 2.6 fusion.171
  28.2 2.8 fusion.172
  32.2 1.7 select_reduce_fusion.3
  33.9 2.6 fusion.171
  36.6 2.8 fusion.172
  40.6 1.7 select_reduce_fusion.3
  42.3 2.6 fusion.171
  44.9 2.8 fusion.172
  48.5 3.4 convolution_convert_fusion.3
  52.2 58.2 %all-reduce.7.cloned.1.call-done = bf16[1536,768]{1,0:T(8,128)(2,1)} async-done(((bf16[1536,768]{1,0:T(8,128)(2,1)}), bf16[1536,768]{1,0:T(8,128)(2,1)}) %all-reduce.7.cloned.1.call-update) | async-done | bytes 2359312 | tf_op jit(solution)/shard_map/psum | solution.py:117
  110.4 3.5 fusion.99
  114.0 3.0 multiply_reduce_fusion.1
  117.0 3.1 add_convert_fusion.2
  121.6 2.1 fusion.103
  123.7 5.3 convert_reduce_fusion.3
  130.4 3.5 convolution_convert_fusion.1
  134.8 3.5 fusion.88
  138.3 7.2 convolution_convert_fusion.2
  145.5 52.9 %all-gather.3.cloned.1.call-done = bf16[6144,768]{1,0:T(8,128)(2,1)} async-done(((bf16[1536,768]{1,0:T(8,128)(2,1)}), bf16[6144,768]{1,0:T(8,128)(2,1)}) %all-gather.3.cloned.1.call-update) | async-done | bytes 9437200 | tf_op jit(solution)/shard_map/all_gather | solution.py:136
  198.4 7.1 reduce_sum.210
  205.5 6.4 fusion.82
  211.9 5.2 fusion.100
  217.2 2.2 copy-done.8
  219.4 1.7 convolution_convert_fusion.4
  224.3 72.2 %while.29 = (s32[]{:T(128)}, f32[1536,3,64]{0,2,1:T(8,128)}, f32[1536,3,64]{0,2,1:T(8,128)S(1)}, bf16[3,512,3,64]{1,3,2,0:T(8,128)(2,1)}, bf16[3,512,3,64]{1,3,2...) while((s32[]{:T(128)}, f32[1536,3,64]{0,2,1:T(8,128)}, ...), condition=%wide.region_16.17_spmd.clone, body=%wide.region_14.16_spmd.clone.sunk | while | flops 1542683648 | bytes 159318784 | solution.py:173
  225.9 1.4 fusion.182
  227.4 4.2 multiply_reduce_fusion.3
  231.6 4.1 multiply_convert_fusion.5
  235.7 4.4 fusion.184
  240.1 4.6 fusion.186
  244.8 3.7 fusion.185
  249.6 1.4 fusion.182
  251.1 4.2 multiply_reduce_fusion.3
  255.3 4.1 multiply_convert_fusion.5
  259.4 4.8 fusion.184
  264.2 4.6 fusion.186
  268.8 3.7 fusion.185
  273.7 1.4 fusion.182
  275.1 4.2 multiply_reduce_fusion.3
  279.4 4.1 multiply_convert_fusion.5
  283.4 4.8 fusion.184
  288.2 4.6 fusion.186
  292.8 3.7 fusion.185
  298.3 2.0 fusion.104
  301.5 2.3 add_convert_fusion
  304.0 6.0 fusion.106
  310.0 6.7 fusion.89
  316.7 1.4 fusion.107
  318.1 1.4 fusion.109
  319.6 1.4 fusion.108
  321.1 1.5 fusion.95
  322.6 75.6 %all-reduce.11.cloned.1.call-done = (bf16[1536,768]{1,0:T(8,128)(2,1)}, bf16[1536,768]{1,0:T(8,128)(2,1)}) async-done(((bf16[1536,768]{1,0:T(8,128)(2,1)}, bf16[1536,768]{1,0:T(8,128)(2,1)}), (bf16[1536,768]{1,0:T(8,128)(2,1)}, bf16[1536,768]{1,0:T(8,128)(2,1)})) %all-reduce.11.cloned.1.call-update) | async-done | bytes 4718608 | tf_op jit(solution)/shard_map/psum | solution.py:124
  398.2 4.6 fusion.83
  402.9 6.9 fusion.101
  409.8 1.9 broadcast_multiply_fusion
  413.1 39.6 %all-reduce = (f32[768]{0:T(1024)}, f32[768]{0:T(1024)}, f32[192]{0:T(256)}, f32[192]{0:T(256)}, f32[768]{0:T(1024)}, /*index=5*/f32[768]{0:T(1024)}, f32[768]{0:T(1024)}, f32[768]{0:T(1024)}, f32[768]{0:T(1024)}) all-reduce(f32[768]{0:T(1024)S(1)} %get-tuple-element.271, ...), channel_id=1, replica_groups=mesh['dp'=8,'tensor'=4] {'dp'}, use_global_device_ids=true, to_apply=%region_23.24 | all-reduce | flops 5760 | bytes 46080 | tf_op jit(solution)/shard_map/psum | solution.py:209
  452.6 282.6 %all-reduce.9.cloned.1.call-done = (f32[1000,768]{1,0:T(8,128)}, f32[768,192]{0,1:T(8,128)}, f32[768,192]{0,1:T(8,128)}, f32[768,192]{0,1:T(8,128)}, f32[192,768...) async-done(((f32[1000,768]{1,0:T(8,128)}, f32[768,192]{0,1:T(8,128)}, f32[768,192]{0,1:T(8,128)}, f32[768,192]{0,1:T(8,128)}, f32[192,768]{1,0:T(8,128)}, ...) | async-done | bytes 10149904 | tf_op jit(solution)/shard_map/psum | solution.py:209
  735.3 3.9 copy.89
  742.4 1.4 copy.94
  (218 shorter events, 31.1 us)
Async XLA Ops:
  7.2 2.1 copy-start
  7.2 5.7 copy-start.43
  7.2 5.7 copy-start.51
  7.2 103.2 %all-reduce.7.cloned.1.call-start = ((), (), s32[]{:S(2)}) async-start(), calls=%async_computation | async-start | bytes 4718592 | tf_op jit(solution)/shard_map/psum | solution.py:117
  7.3 4.6 copy-start.4
  9.6 6.1 copy-start.35
  9.7 6.0 copy-start.60
  11.9 122.9 %copy-start.33 = (f32[1536]{0:T(1024)}, f32[1536]{0:T(1024)S(1)}, u32[]{:S(2)}) copy-start(f32[1536]{0:T(1024)S(1)} %broadcast_multiply_fusion.7) | copy-start | bytes 18436
  12.9 121.9 %copy-start.40 = (f32[1536]{0:T(1024)}, f32[1536]{0:T(1024)S(1)}, u32[]{:S(2)}) copy-start(f32[1536]{0:T(1024)S(1)} %add_rsqrt_fusion.1) | copy-start | bytes 18436
  15.7 1.5 copy-start.36
  16.6 3.2 copy-start.55
  16.6 3.3 copy-start.38
  16.7 3.3 copy-start.61
  47.8 66.2 %copy-start.11 = (bf16[1536,3,64]{0,2,1:T(8,128)(2,1)}, bf16[1536,3,64]{0,2,1:T(8,128)(2,1)S(1)}, u32[]{:S(2)}) copy-start(bf16[1536,3,64]{0,2,1:T(8,128)(2,1)S(1)} %get-tuple-element.617) | copy-start | bytes 1769476
  47.8 62.6 %copy-start.42 = (f32[768]{0:T(1024)S(1)}, f32[768]{0:T(1024)}, u32[]{:S(2)}) copy-start(f32[768]{0:T(1024)} %param.36) | copy-start | bytes 9220
  48.5 65.5 %copy-start.15 = (bf16[24,8,3,512]{3,1,2,0:T(8,128)(2,1)}, bf16[24,8,3,512]{3,1,2,0:T(8,128)(2,1)S(1)}, u32[]{:S(2)}) copy-start(bf16[24,8,3,512]{3,1,2,0:T(8,128)(2,1)S(1)} %copy.51) | copy-start | bytes 1769476
  51.9 65.1 %copy-start.45 = (f32[768]{0:T(1024)S(1)}, f32[768]{0:T(1024)}, u32[]{:S(2)}) copy-start(f32[768]{0:T(1024)} %param.37) | copy-start | bytes 9220
  51.9 65.1 %copy-start.52 = (f32[768]{0:T(1024)S(1)}, f32[768]{0:T(1024)}, u32[]{:S(2)}) copy-start(f32[768]{0:T(1024)} %param.38) | copy-start | bytes 9220
  51.9 146.5 %all-gather.3.cloned.1.call-start = ((), (), s32[]{:S(2)}) async-start(), calls=%async_computation.1 | async-start | bytes 11796480 | tf_op jit(solution)/shard_map/all_gather | solution.py:136
  110.4 3.5 copy-start.6
  117.0 4.6 copy-start.56
  121.6 2.1 copy-start.21
  121.6 2.1 copy-start.57
  121.6 2.1 copy-start.59
  123.7 5.3 copy-start.62
  133.9 264.2 %all-reduce.11.cloned.1.call-start = ((), (), s32[]{:S(2)}) async-start(), calls=%async_computation.3 | async-start | bytes 9437184 | tf_op jit(solution)/shard_map/psum | solution.py:124
  134.2 4.1 copy-start.58
  205.5 6.4 copy-start.5
  205.5 6.4 copy-start.7
  205.5 6.4 copy-start.10
  211.9 7.5 copy-start.28
  217.2 2.2 copy-start.8
  227.4 4.3 copy-start.2
  235.7 9.1 %copy-start.3 = (f32[3,512,1536]{2,1,0:T(8,128)S(1)}, f32[3,512,1536]{2,1,0:T(8,128)}, u32[]{:S(2)}) copy-start(f32[3,512,1536]{2,1,0:T(8,128)} %copy-done.2) | copy-start | bytes 28311556 | tf_op jit(solution)/shard_map/while
  249.6 1.5 copy-start.12
  251.1 4.3 copy-start.2
  259.4 9.4 %copy-start.3 = (f32[3,512,1536]{2,1,0:T(8,128)S(1)}, f32[3,512,1536]{2,1,0:T(8,128)}, u32[]{:S(2)}) copy-start(f32[3,512,1536]{2,1,0:T(8,128)} %copy-done.2) | copy-start | bytes 28311556 | tf_op jit(solution)/shard_map/while
  273.6 1.5 copy-start.12
  275.1 4.3 copy-start.2
  283.4 9.4 %copy-start.3 = (f32[3,512,1536]{2,1,0:T(8,128)S(1)}, f32[3,512,1536]{2,1,0:T(8,128)}, u32[]{:S(2)}) copy-start(f32[3,512,1536]{2,1,0:T(8,128)} %copy-done.2) | copy-start | bytes 28311556 | tf_op jit(solution)/shard_map/while
  298.3 2.1 copy-start.18
  298.3 2.1 copy-start.9
  298.3 2.1 copy-start.37
  303.8 431.5 %all-reduce.9.cloned.1.call-start = ((), (), s32[]{:S(2)}) async-start(), calls=%async_computation.2 | async-start | bytes 20299776 | tf_op jit(solution)/shard_map/psum | solution.py:209
  304.0 6.0 copy-start.22
  310.0 6.7 copy-start.19
  310.0 6.7 copy-start.26
  316.7 4.4 slice-start
  318.1 2.9 slice-start.1
  318.1 2.9 copy-start.16
  319.6 78.6 %copy-start.34 = (f32[1536]{0:T(1024)S(1)}, f32[1536]{0:T(1024)}, u32[]{:S(2)}) copy-start(f32[1536]{0:T(1024)} %copy-done.33) | copy-start | bytes 18436
  319.6 78.6 %copy-start.41 = (f32[1536]{0:T(1024)S(1)}, f32[1536]{0:T(1024)}, u32[]{:S(2)}) copy-start(f32[1536]{0:T(1024)} %copy-done.40) | copy-start | bytes 18436
  319.6 78.6 %copy-start.44 = (f32[768]{0:T(1024)S(1)}, f32[768]{0:T(1024)}, u32[]{:S(2)}) copy-start(f32[768]{0:T(1024)} %param.28) | copy-start | bytes 9220
  321.1 81.8 %copy-start.53 = (f32[768]{0:T(1024)S(1)}, f32[768]{0:T(1024)}, u32[]{:S(2)}) copy-start(f32[768]{0:T(1024)} %param.42) | copy-start | bytes 9220
  398.2 4.7 copy-start.13
  398.2 4.7 copy-start.20
  402.8 6.9 copy-start.50
  735.2 3.9 copy-start.32
  735.3 4.7 copy-start.31
  735.3 5.5 copy-start.30
  735.3 6.3 copy-start.29
  735.3 7.1 copy-start.25
  739.1 4.7 copy-start.24
  741.6 3.6 copy-start.1
  (11 other events, 14.5 us)
Sparse Core Ops, SparseCore 0:
  52.0 58.3 all-reduce.6
  134.0 64.3 all-gather.2
  303.9 94.2 all-reduce.10
  411.9 323.3 all-reduce.8
